TPU v7x, 32 devices: a whole 2x2x4 slice. The times are simulated.
32 devices in a mesh: rows: 2 (over x), cols: 4 (over y, core), dp: 4 (over z).
Axes of the slice: x: 2, y: 2, z: 4, core: 2. Of those that a mesh axis runs over, the one named last changes fastest.
Arguments:
- fields: float32 [128, 64, 384], P(('dp', 'rows'), 'cols'), parts along dimension 0, may hold values from -6 to 6
- logit_scale: float32 [6], replicated, may hold values from 4 to 25
- w_qkv: bfloat16 [384, 1152], replicated, may hold values from -0.3125 to 0.3125
- w_proj: bfloat16 [384, 384], replicated, may hold values from -0.3125 to 0.3125
- w_merge: bfloat16 [1536, 768], P(None, 'cols'), may hold values from -0.15625 to 0.15625
- w_up: bfloat16 [768, 3072], P('rows', 'cols'), may hold values from -0.21875 to 0.21875
- w_down: bfloat16 [3072, 768], P('cols', 'rows'), may hold values from -0.109375 to 0.109375
- cotangent: bfloat16 [64, 32, 768], P(('dp', 'rows'), 'cols'), parts along dimension 0, may hold values from -0.59765625 to 0.59765625
Outputs:
- coarse: float32 [64, 32, 768], P(('dp', 'rows'), 'cols'), parts along dimension 0
- grad_coarse: float32 [64, 32, 768], P(('dp', 'rows'), 'cols'), parts along dimension 0
- grad_up: float32 [768, 12288], P('rows', ('dp', 'cols')), parts along dimension 1
- grad_down: float32 [3072, 3072], P('cols', ('dp', 'rows')), parts along dimension 1
There are 4 independent parts, one for each index of `dp`. A program takes and returns all parts, laid end to end along the dimension named above; an argument that names none is the same for every part. Nothing has to cross between parts.
All inputs are finite; a program needn't handle non-finite values.
Results may differ from a plain program's by a relative error of at most 0.02.
Values may be sent and summed in bfloat16 or wider, within the bound.
A program may use at most 64 MiB of HBM per device.

v0:
```python
import jax
import jax.numpy as jnp
from jax import lax
from jax.sharding import PartitionSpec as P

WIN = 16


eps_norm = 1e-05
eps_unit = 1e-06


def padded_2(cells, sides, width):
    for axis, dim in sides:
        count = lax.axis_size(axis)
        head = lax.slice_in_dim(cells, 0, width, axis=dim)
        tail = lax.slice_in_dim(cells, cells.shape[dim] - width, cells.shape[dim], axis=dim)
        cells = jnp.concatenate(
            [
                lax.ppermute(tail, axis, [(i, (i + 1) % count) for i in range(count)]),
                cells,
                lax.ppermute(head, axis, [((i + 1) % count, i) for i in range(count)]),
            ],
            axis=dim,
        )
    return cells


def layer_norm(value):
    average = jnp.mean(value, axis=-1, keepdims=True)
    centred = value - average
    spread = jnp.mean(centred * centred, axis=-1, keepdims=True)
    inverse = lax.rsqrt(spread + eps_norm)
    return (centred * inverse, inverse)


def norm_slope(upstream, normed, inverse):
    first_mean = jnp.mean(upstream, axis=-1, keepdims=True)
    second_mean = jnp.mean(upstream * normed, axis=-1, keepdims=True)
    return inverse * (upstream - first_mean - normed * second_mean)


def unit_heads(value, head_count):
    shaped = value.reshape(value.shape[:-1] + (head_count, value.shape[-1] // head_count))
    squares = jnp.sum(shaped * shaped, axis=-1, keepdims=True)
    return (shaped * lax.rsqrt(squares + eps_unit)).reshape(value.shape)


def windows_of(field_grid, window):
    grid_rows, grid_cols, channels = field_grid.shape
    shaped = field_grid.reshape(grid_rows // window, window, grid_cols // window, window, channels)
    return shaped.transpose(0, 2, 1, 3, 4).reshape(-1, window * window, channels)


def grid_of(blocks, grid_rows, grid_cols, window):
    channels = blocks.shape[-1]
    shaped = blocks.reshape(grid_rows // window, grid_cols // window, window, window, channels)
    return shaped.transpose(0, 2, 1, 3, 4).reshape(grid_rows, grid_cols, channels)


def attend(queries, key_rows, value_rows, logit_scale, head_count):
    number, window_size, channels = queries.shape
    width_head = channels // head_count
    query_heads = queries.reshape(number, window_size, head_count, width_head)
    key_heads = key_rows.reshape(number, window_size, head_count, width_head)
    value_heads = value_rows.reshape(number, window_size, head_count, width_head)
    scores = jnp.einsum(
        "wqhd,wkhd->whqk", query_heads, key_heads, preferred_element_type=jnp.float32
    )
    weights = jnp.exp(scores * logit_scale[None, :, None, None])
    weights = (weights / jnp.sum(weights, axis=-1, keepdims=True)).astype(jnp.bfloat16)
    mixed_out = jnp.einsum(
        "whqk,wkhd->wqhd", weights, value_heads, preferred_element_type=jnp.float32
    )
    return mixed_out.reshape(number, window_size, channels)


def merge_patches(field_grid):
    quarters = (
        field_grid[0::2, 0::2],
        field_grid[1::2, 0::2],
        field_grid[0::2, 1::2],
        field_grid[1::2, 1::2],
    )
    return jnp.concatenate(quarters, axis=-1)


def exact_gelu(value):
    return jax.nn.gelu(value, approximate=False)


def local(fields, logit_scale, w_qkv, w_proj, w_merge, w_up, w_down, cotangent):
    tile_rows, tile_cols, channels = fields.shape
    offset = WIN // 2
    head_count = logit_scale.shape[0]
    tokens = fields.astype(jnp.bfloat16)
    token_rows = tokens.reshape(-1, channels)
    wide_rows = tile_rows + WIN
    wide_cols = tile_cols + WIN
    widened = padded_2(tokens, (("rows", 0), ("cols", 1)), offset)
    wide_proj = jnp.dot(
        widened.reshape(-1, channels), w_qkv[:, channels:], preferred_element_type=jnp.float32
    )
    key_grid = unit_heads(wide_proj[:, :channels], head_count).astype(jnp.bfloat16)
    value_grid = wide_proj[:, channels:].astype(jnp.bfloat16)
    query_raw = jnp.dot(token_rows, w_qkv[:, :channels], preferred_element_type=jnp.float32)
    queries = (
        unit_heads(query_raw, head_count)
        .astype(jnp.bfloat16)
        .reshape(tile_rows, tile_cols, channels)
    )
    padded = jnp.pad(queries, ((offset, offset), (offset, offset), (0, 0)))
    key_blocks = windows_of(key_grid.reshape(wide_rows, wide_cols, channels), WIN)
    value_blocks = windows_of(value_grid.reshape(wide_rows, wide_cols, channels), WIN)
    mixed = attend(windows_of(padded, WIN), key_blocks, value_blocks, logit_scale, head_count)
    mixed = grid_of(mixed, wide_rows, wide_cols, WIN)[
        offset : offset + tile_rows, offset : offset + tile_cols
    ]
    mixed = mixed.astype(jnp.bfloat16).reshape(-1, channels)
    normed, _ = layer_norm(jnp.dot(mixed, w_proj, preferred_element_type=jnp.float32))
    stream = fields + normed.reshape(fields.shape)
    merged = merge_patches(stream).astype(jnp.bfloat16)
    merged_rows = merged.reshape(-1, merged.shape[-1])
    own_count = merged_rows.shape[0]
    partial_band = jnp.dot(
        lax.all_gather(merged_rows, "cols", axis=0, tiled=True),
        w_merge,
        preferred_element_type=jnp.float32,
    )
    projected_band = lax.all_gather(
        partial_band.astype(jnp.bfloat16), "cols", axis=1, tiled=True
    ).astype(partial_band.dtype)
    level_band, _ = layer_norm(projected_band)
    level_b = level_band.astype(jnp.bfloat16)
    level_own = lax.dynamic_slice_in_dim(
        level_band, lax.axis_index("cols") * own_count, own_count, 0
    )
    up_full = lax.all_gather(w_up, "rows", axis=0, tiled=True)
    down_full = lax.all_gather(w_down, "rows", axis=1, tiled=True)
    hidden_pre = jnp.dot(level_b, up_full, preferred_element_type=jnp.float32)
    hidden = exact_gelu(hidden_pre).astype(jnp.bfloat16)
    rows_part = hidden
    branch_out = lax.psum_scatter(
        jnp.dot(rows_part, down_full, preferred_element_type=jnp.float32).astype(jnp.bfloat16),
        "cols",
        scatter_dimension=0,
        tiled=True,
    ).astype(jnp.float32)
    branch_norm, branch_inv = layer_norm(branch_out)
    coarse = level_own + branch_norm
    upstream = cotangent.astype(jnp.float32).reshape(own_count, -1)
    slope_own = norm_slope(upstream, branch_norm, branch_inv).astype(jnp.bfloat16)
    slope_out = lax.all_gather(slope_own, "cols", axis=0, tiled=True)
    slope_hidden = jnp.einsum("tc,fc->tf", slope_out, down_full, preferred_element_type=jnp.float32)
    _, pullback = jax.vjp(exact_gelu, hidden_pre)
    slope_pre = pullback(slope_hidden)[0].astype(jnp.bfloat16)
    rows_part = slope_pre
    slope_input = lax.psum_scatter(
        jnp.einsum("tf,cf->tc", rows_part, up_full, preferred_element_type=jnp.float32).astype(
            jnp.bfloat16
        ),
        "cols",
        scatter_dimension=0,
        tiled=True,
    ).astype(jnp.float32)
    grad_coarse = upstream + slope_input
    term_up = jnp.einsum("tc,tf->cf", level_b, slope_pre, preferred_element_type=jnp.float32)
    term_down = jnp.einsum("tf,tc->fc", hidden, slope_out, preferred_element_type=jnp.float32)
    grad_up, grad_down = (
        lax.psum_scatter(
            term_up.astype(jnp.bfloat16), "rows", scatter_dimension=0, tiled=True
        ).astype(jnp.float32),
        lax.psum_scatter(
            term_down.astype(jnp.bfloat16), "rows", scatter_dimension=1, tiled=True
        ).astype(jnp.float32),
    )
    coarse_shape = (tile_rows // 2, tile_cols // 2, coarse.shape[-1])
    return (coarse.reshape(coarse_shape), grad_coarse.reshape(coarse_shape), grad_up, grad_down)


def solution(mesh):
    return jax.shard_map(
        local,
        mesh=mesh,
        in_specs=(
            P(("dp", "rows"), "cols", None),
            P(),
            P(),
            P(),
            P(None, "cols"),
            P("rows", "cols"),
            P("cols", "rows"),
            P(("dp", "rows"), "cols", None),
        ),
        out_specs=(
            P(("dp", "rows"), "cols", None),
            P(("dp", "rows"), "cols", None),
            P("rows", ("dp", "cols")),
            P("cols", ("dp", "rows")),
        ),
        check_vma=False,
    )
```

profile of v0, /device:TPU:0, one launch (start us, length us, event | category | flops | bytes accessed | tf_op | source)
XLA Modules:
  0.0 198.9 jit_solution(13861264491518459339)
XLA Ops:
  9.0 3.0 %collective-permute-start = (bf16[8,16,384]{2,1,0:T(8,128)(2,1)S(1)}, bf16[8,16,384]{2,1,0:T(8,128)(2,1)S(1)}, u32[]{:S(2)}, u32[]{:S(2)}) collective-permute-start(bf16[8,16,384]{2,1,0:T(8,128)(2,1)S(1)} %get-tuple-element.12), channel_id=1, source_target_pairs={{0,16},{16,0},{1,17},{17,1},{2,18},{18,2},{3,19},{19,3},{4,20},{20... | collective-permute-start | bytes 294920 | tf_op jit(solution)/shard_map/ppermute | solution.py:20
  13.7 1.7 collective-permute-done
  15.5 1.5 collective-permute-done.1
  17.8 1.7 collective-permute-start.3
  21.3 2.7 %reshape_reshape.21 = bf16[4,256,6,64]{3,2,1,0:T(8,128)(2,1)S(1)} reshape(bf16[2,2,16,16,384]{4,3,2,1,0:T(8,128)(2,1)} %copy.76) | data formatting | bytes 1572864 | tf_op jit(solution)/shard_map/reshape;reshape | solution.py:64
  26.1 1.3 slice_multiply_fusion
  28.3 3.1 %copy.77 = f32[1024,384]{0,1:T(8,128)} copy(f32[1024,384]{1,0:T(8,128)} %slice_multiply_fusion) | data formatting | bytes 3145728 | tf_op jit(solution)/shard_map/mul | solution.py:45
  31.4 1.6 reduce_sum.100
  33.0 1.4 mul.126
  34.3 3.0 %copy.78 = f32[1024,384]{1,0:T(8,128)} copy(f32[1024,384]{0,1:T(8,128)} %bitcast.75) | data formatting | bytes 3145728 | tf_op jit(solution)/shard_map/mul | solution.py:46
  37.4 2.0 %multiply_convert_fusion = bf16[1024,384]{1,0:T(8,128)(2,1)S(1)} fusion(f32[1024,384]{1,0:T(8,128)} %copy.78, f32[1024,768]{1,0:T(8,128)} %copy-done.1), kind=kLoop, calls=%fused_computation.9 | loop fusion | flops 786432 | bytes 3932160 | tf_op jit(solution)/shard_map/convert_element_type | solution.py:104
  40.3 3.8 %reshape_reshape.23 = bf16[4,256,6,64]{3,2,1,0:T(8,128)(2,1)} reshape(bf16[2,2,16,16,384]{4,3,2,1,0:T(8,128)(2,1)} %bitcast.80) | data formatting | bytes 1572864 | tf_op jit(solution)/shard_map/reshape;reshape | solution.py:65
  45.1 3.8 %reshape_reshape.20 = bf16[4,256,6,64]{3,2,1,0:T(8,128)(2,1)} reshape(bf16[2,2,16,16,384]{4,3,2,1,0:T(8,128)(2,1)} %bitcast.81) | data formatting | bytes 1572864 | tf_op jit(solution)/shard_map/reshape;reshape | solution.py:66
  48.9 3.0 %fusion = (f32[4,6,256]{2,1,0:T(8,128)S(1)}, f32[4,6,256,256]{2,3,1,0:T(8,128)S(1)}) fusion(f32[6]{0:T(128)S(1)} %copy-done.8, bf16[4,256,6,64]{3,2,1,0:T(8,128)(2,1)} %reshape_reshape.23, bf16[4,256,6,64]{3,2,1,0:T(8,128)(2,1)S(1)} %reshape_reshape.21), kind=kOutput, calls=%fused_computation.2 | convolution fusion | flops 204466176 | bytes 7888920 | tf_op jit(solution)/shard_map/wqhd,wkhd->whqk/dot_general | solution.py:67
  51.9 1.3 fusion.9
  58.9 9.1 %all_gather.15 = bf16[256,1536]{1,0:T(8,128)(2,1)S(1)} all-gather(bf16[64,1536]{1,0:T(8,128)(2,1)S(1)} %pad_maximum_fusion.2), channel_id=1, replica_groups=mesh['rows'=2,'cols'=4,'dp'=4] {'cols'}, dimensions={0}, use_global_device_ids=true | all-gather | bytes 983040 | tf_op jit(solution)/shard_map/all_gather | solution.py:126
  68.4 6.6 %all_gather.16 = bf16[256,768]{0,1:T(8,128)(2,1)S(1)} all-gather(bf16[256,192]{0,1:T(8,128)(2,1)S(1)} %convolution_convert_fusion.4), channel_id=1, replica_groups=mesh['rows'=2,'cols'=4,'dp'=4] {'cols'}, dimensions={1}, use_global_device_ids=true | all-gather | bytes 491520 | tf_op jit(solution)/shard_map/all_gather | solution.py:130
  75.6 4.3 %multiply_convert_fusion.1 = (bf16[256,768]{1,0:T(8,128)(2,1)S(1)}, f32[256,768]{1,0:T(8,128)}, f32[256,768]{1,0:T(8,128)}) fusion(bf16[768,768]{1,0:T(8,128)(2,1)} %all-gather.3.cloned.1.call-done, f32[256]{0:T(256)S(1)} %add_rsqrt_fusion.2, f32[256]{0:T(256)S(1)} %broadcast_multiply_fusion.1, bf16[256,768]{1,0:T(8,128)(2,1)S(1)} %copy.86), kind=kOutput, calls=%fused_computation.29 | convolution fusion | flops 315555840 | bytes 3540992 | tf_op jit(solution)/shard_map/dot_general | solution.py:140
  79.9 2.5 %convolution_convert_fusion.3 = bf16[256,768]{1,0:T(8,128)(2,1)} fusion(bf16[256,768]{1,0:T(8,128)(2,1)S(1)} %get-tuple-element.8, bf16[768,768]{1,0:T(8,128)(2,1)} %all-gather.5.cloned.1.call-done), kind=kOutput, calls=%fused_computation.16 | convolution fusion | flops 302186496 | bytes 1966080 | tf_op jit(solution)/shard_map/dot_general | solution.py:144
  82.9 21.8 %reduce-scatter.13.cloned.1.call-done = bf16[64,768]{1,0:T(8,128)(2,1)} async-done(((bf16[256,768]{1,0:T(8,128)(2,1)}), bf16[64,768]{1,0:T(8,128)(2,1)}) %reduce-scatter.13.cloned.1.call-update) | async-done | bytes 98320 | tf_op jit(solution)/shard_map/reduce_scatter | solution.py:143
  108.0 1.7 fusion.33
  109.7 6.1 %all_gather.19 = bf16[256,768]{1,0:T(8,128)(2,1)S(1)} all-gather(bf16[64,768]{1,0:T(8,128)(2,1)S(1)} %get-tuple-element.14), channel_id=1, replica_groups=mesh['rows'=2,'cols'=4,'dp'=4] {'cols'}, dimensions={0}, use_global_device_ids=true | all-gather | bytes 491520 | tf_op jit(solution)/shard_map/all_gather | solution.py:153
  115.8 2.4 %add_convert_fusion = bf16[256,768]{1,0:T(8,128)(2,1)S(1)} fusion(f32[256,768]{1,0:T(8,128)} %get-tuple-element.9, f32[256,768]{1,0:T(8,128)} %get-tuple-element.22, bf16[256,768]{1,0:T(8,128)(2,1)S(1)} %all_gather.19, bf16[768,768]{1,0:T(8,128)(2,1)} %all-gather.5.cloned.1.call-done), kind=kOutput, calls=%fused_computation.28 | convolution fusion | flops 304742400 | bytes 3538944 | tf_op jit(solution)/shard_map/tc,fc->tf/dot_general | solution.py:154
  118.3 1.3 convolution_convert_fusion.2
  120.1 1.5 copy.92
  121.7 1.7 convolution_convert_fusion.1
  123.4 17.5 %reduce-scatter.9.cloned.1.call-done = bf16[64,768]{1,0:T(8,128)(2,1)} async-done(((bf16[256,768]{1,0:T(8,128)(2,1)}), bf16[64,768]{1,0:T(8,128)(2,1)}) %reduce-scatter.9.cloned.1.call-update) | async-done | bytes 98320 | tf_op jit(solution)/shard_map/reduce_scatter | solution.py:158
  140.8 1.6 fusion.36
  142.4 22.9 %reduce-scatter.15.cloned.1.call-done = bf16[384,768]{1,0:T(8,128)(2,1)} async-done(((bf16[768,768]{1,0:T(8,128)(2,1)}), bf16[384,768]{1,0:T(8,128)(2,1)}) %reduce-scatter.15.cloned.1.call-update) | async-done | bytes 589840
  165.4 1.4 copy.93
  167.8 22.1 %reduce-scatter.11.cloned.1.call-done = bf16[384,768]{1,0:T(8,128)(2,1)} async-done(((bf16[768,768]{1,0:T(8,128)(2,1)}), bf16[384,768]{1,0:T(8,128)(2,1)}) %reduce-scatter.11.cloned.1.call-update) | async-done | bytes 589840 | tf_op jit(solution)/shard_map/reduce_scatter | solution.py:170
  189.9 2.2 %convert_element_type.84 = f32[384,768]{1,0:T(8,128)} convert(bf16[384,768]{1,0:T(8,128)(2,1)} %reduce-scatter.11.cloned.1.call-done) | non-fusion elementwise | flops 294912 | bytes 1769472 | tf_op jit(solution)/shard_map/convert_element_type | solution.py:172
  (88 shorter events, 22.9 us)
Async XLA Ops:
  7.2 60.8 %copy-start = (bf16[1536,192]{0,1:T(8,128)(2,1)S(1)}, bf16[1536,192]{0,1:T(8,128)(2,1)}, u32[]{:S(2)}) copy-start(bf16[1536,192]{0,1:T(8,128)(2,1)} %param.12) | copy-start | bytes 1769476
  7.2 68.4 %all-gather.3.cloned.1.call-start = ((), (), s32[]{:S(2)}) async-start(), calls=%async_computation.4 | async-start | bytes 1769472 | tf_op jit(solution)/shard_map/all_gather | solution.py:138
  7.9 72.0 %all-gather.5.cloned.1.call-start = ((), (), s32[]{:S(2)}) async-start(), calls=%async_computation.5 | async-start | bytes 1769472 | tf_op jit(solution)/shard_map/all_gather | solution.py:139
  9.0 6.5 %collective-permute-start = (bf16[8,16,384]{2,1,0:T(8,128)(2,1)S(1)}, bf16[8,16,384]{2,1,0:T(8,128)(2,1)S(1)}, u32[]{:S(2)}, u32[]{:S(2)}) collective-permute-start(bf16[8,16,384]{2,1,0:T(8,128)(2,1)S(1)} %get-tuple-element.12), channel_id=1, source_target_pairs={{0,16},{16,0},{1,17},{17,1},{2,18},{18,2},{3,19},{19,3},{4,20},{20... | collective-permute-start | bytes 294920 | tf_op jit(solution)/shard_map/ppermute | solution.py:20
  12.0 4.9 %collective-permute-start.1 = (bf16[8,16,384]{2,1,0:T(8,128)(2,1)S(1)}, bf16[8,16,384]{2,1,0:T(8,128)(2,1)S(1)}, u32[]{:S(2)}, u32[]{:S(2)}) collective-permute-start(bf16[8,16,384]{2,1,0:T(8,128)(2,1)S(1)} %get-tuple-element.13), channel_id=1, source_target_pairs={{16,0},{0,16},{17,1},{1,17},{18,2},{2,18},{19,3},{3,19},{20,4},{4,... | collective-permute-start | bytes 294920 | tf_op jit(solution)/shard_map/ppermute | solution.py:22
  12.2 92.6 %reduce-scatter.13.cloned.1.call-start = ((), (), s32[]{:S(2)}) async-start(), calls=%async_computation.8 | async-start | bytes 491520 | tf_op jit(solution)/shard_map/reduce_scatter | solution.py:143
  17.8 6.2 %collective-permute-start.2 = (bf16[32,8,384]{2,1,0:T(8,128)(2,1)}, bf16[32,8,384]{2,1,0:T(8,128)(2,1)S(1)}, u32[]{:S(2)}, u32[]{:S(2)}) collective-permute-start(bf16[32,8,384]{2,1,0:T(8,128)(2,1)} %get-tuple-element.10), channel_id=1, source_target_pairs={{0,4},{4,8},{8,12},{12,0},{1,5},{5,9},{9,13},{13,1},{2,6},{6,10},{... | collective-permute-start | bytes 589832 | tf_op jit(solution)/shard_map/ppermute | solution.py:20
  17.8 6.9 %collective-permute-start.3 = (bf16[32,8,384]{2,1,0:T(8,128)(2,1)}, bf16[32,8,384]{2,1,0:T(8,128)(2,1)S(1)}, u32[]{:S(2)}, u32[]{:S(2)}) collective-permute-start(bf16[32,8,384]{2,1,0:T(8,128)(2,1)} %get-tuple-element.11), channel_id=1, source_target_pairs={{4,0},{8,4},{12,8},{0,12},{5,1},{9,5},{13,9},{1,13},{6,2},{10,6},{... | collective-permute-start | bytes 589832 | tf_op jit(solution)/shard_map/ppermute | solution.py:22
  24.0 1.2 copy-start.6
  26.1 2.1 %copy-start.1 = (f32[1024,768]{1,0:T(8,128)}, f32[1024,768]{1,0:T(8,128)S(1)}, u32[]{:S(2)}) copy-start(f32[1024,768]{1,0:T(8,128)S(1)} %fusion.21) | copy-start | bytes 9437188
  45.1 3.8 %copy-start.8 = (f32[6]{0:T(128)S(1)}, f32[6]{0:T(128)}, u32[]{:S(2)}) copy-start(f32[6]{0:T(128)} %param.9) | copy-start | bytes 76
  48.9 3.0 %copy-start.2 = (bf16[4,256,6,64]{3,2,1,0:T(8,128)(2,1)S(1)}, bf16[4,256,6,64]{3,2,1,0:T(8,128)(2,1)}, u32[]{:S(2)}) copy-start(bf16[4,256,6,64]{3,2,1,0:T(8,128)(2,1)} %reshape_reshape.20) | copy-start | bytes 2359300
  55.7 1.0 copy-start.7
  55.8 1.6 copy-start.4
  79.9 2.6 %copy-start.3 = (bf16[8,8,768]{2,1,0:T(8,128)(2,1)S(1)}, bf16[8,8,768]{2,1,0:T(8,128)(2,1)}, u32[]{:S(2)}) copy-start(bf16[8,8,768]{2,1,0:T(8,128)(2,1)} %param.15) | copy-start | bytes 294916
  82.5 58.3 %reduce-scatter.9.cloned.1.call-start = ((), (), s32[]{:S(2)}) async-start(), calls=%async_computation.6 | async-start | bytes 491520 | tf_op jit(solution)/shard_map/reduce_scatter | solution.py:158
  115.8 2.4 %copy-start.5 = (bf16[768,768]{1,0:T(8,128)(2,1)S(1)}, bf16[768,768]{1,0:T(8,128)(2,1)}, u32[]{:S(2)}) copy-start(bf16[768,768]{1,0:T(8,128)(2,1)} %all-gather.3.cloned.1.call-done) | copy-start | bytes 3538948
  119.6 45.8 %reduce-scatter.15.cloned.1.call-start = ((), (), s32[]{:S(2)}) async-start(), calls=%async_computation.9 | async-start | bytes 1769472
  121.6 68.3 %reduce-scatter.11.cloned.1.call-start = ((), (), s32[]{:S(2)}) async-start(), calls=%async_computation.7 | async-start | bytes 1769472 | tf_op jit(solution)/shard_map/reduce_scatter | solution.py:170
Sparse Core Ops, SparseCore 0:
  9.5 25.4 all-gather.2
  36.6 22.7 all-gather.4
  82.6 22.0 reduce-scatter.12
  119.7 21.0 reduce-scatter.8
  143.5 21.8 reduce-scatter.14
  168.0 21.8 reduce-scatter.10
where the time goes:
time: 200 us; the launch traced here: 199 us
  waiting for transfers between devices  89 us (44%)
  local copies, waits for them, and re-layouts  32.4 us (16%)
  blocking collectives  21.8 us (11%)
  matrix products  19.1 us (10%)
  other arithmetic  17 us (8%)
  between operations  14.5 us (7%)
  starting transfers between devices  5.1 us (3%)
    unnamed x7, waiting for transfers between devices  23.7 us
    reduce_scatter x1, waiting for transfers between devices, local(): lax.psum_scatter(term_up.astype(jnp.bfloat16), 'rows', scatter_dimension=...  22.1 us
    reduce_scatter x1, waiting for transfers between devices, local(): lax.psum_scatter(jnp.dot(rows_part, down_full, preferred_element_type=jnp...  21.8 us
    reduce_scatter x1, waiting for transfers between devices, local(): lax.psum_scatter(jnp.einsum('tf,cf->tc', rows_part, up_full, preferred_el...  17.5 us
    all_gather x1, blocking collectives, local(): lax.all_gather(merged_rows, 'cols', axis=0, tiled=True)  9.13 us
    all_gather x1, blocking collectives, local(): lax.all_gather(partial_band.astype(jnp.bfloat16), 'cols', axis=1, tiled=T...  6.58 us
    all_gather x1, blocking collectives, local(): slope_out = lax.all_gather(slope_own, 'cols', axis=0, tiled=True)  6.12 us
    unnamed x20, local copies, waits for them, and re-layouts  4.86 us
  transfers between devices with their start and end apart: 10, of which 7 were waited for; matrix products, arithmetic and copies ran while one was open for 27% of the time, Pallas kernels for 0%

commit v1 on v0

--- a/solution.py
+++ b/solution.py
@@ -1,6 +1,9 @@
 import jax
 import jax.numpy as jnp
+import numpy as np
 from jax import lax
+from jax.experimental import pallas as pl
+from jax.experimental.pallas import tpu as pltpu
 from jax.sharding import PartitionSpec as P
 
 WIN = 16
@@ -178,9 +181,330 @@
     return (coarse.reshape(coarse_shape), grad_coarse.reshape(coarse_shape), grad_up, grad_down)
 
 
+def _ln(value):
+    average = jnp.mean(value, axis=-1, keepdims=True)
+    centred = value - average
+    spread = jnp.mean(centred * centred, axis=-1, keepdims=True)
+    inverse = lax.rsqrt(spread + eps_norm)
+    return centred * inverse, inverse
+
+
+def _dot(a, b, ca=1, cb=0):
+    return lax.dot_general(
+        a, b, (((ca,), (cb,)), ((), ())), preferred_element_type=jnp.float32
+    )
+
+
+def fused_kernel(
+    fields, logit, w_qkv, w_proj, w_merge, w_up, w_down, cot,
+    coarse, gcoarse, gup, gdown,
+    sendq, winq, mixw, mixq, wm, up, down, lvl, hid, dgel, bsend, brecv, slo, spre, gsend, grecv,
+    lvl_p, hid_p, slo_p, spre_p,
+    loc, s_q, r_q, s_b, r_b, s_w, r_w, s_l, r_l, s_d, r_d, s_s, r_s, s_g, r_g, s_p, r_p,
+):
+    f32, bf16 = jnp.float32, jnp.bfloat16
+    i, j = lax.axis_index("rows"), lax.axis_index("cols")
+    ni, nj = lax.axis_size("rows"), lax.axis_size("cols")
+    half_side = WIN // 2
+    quad = half_side * half_side
+    ch = fields.shape[-1]
+    c4 = cot.shape[-1]
+    own = cot.shape[0]
+    half = c4 // ni
+    heads = logit.shape[0]
+    width = ch // heads
+    other = (i + 1) % ni
+    prev_j, next_j = (j + nj - 1) % nj, (j + 1) % nj
+    partner = j + 1 - 2 * (j % 2)
+    far = (j + 2) % nj
+    far_partner = (partner + 2) % nj
+    peers = (partner, far, far_partner)
+
+    def remote(src, dst, send, recv, row, col):
+        return pltpu.make_async_remote_copy(
+            src_ref=src, dst_ref=dst, send_sem=send, recv_sem=recv,
+            device_id={"rows": row, "cols": col}, device_id_type=pl.DeviceIdType.MESH,
+        )
+
+    def quarter(a, b):
+        part = fields[a * half_side:(a + 1) * half_side, b * half_side:(b + 1) * half_side, :]
+        return part.reshape(quad, ch)
+
+    for k in range(3):
+        sendq[k] = quarter(k // 2, k % 2).astype(bf16)
+    winq[3] = quarter(1, 1).astype(bf16)
+
+    barrier = pltpu.get_barrier_semaphore()
+    greet = [(i, p) for p in peers] + [(other, j), (other, prev_j), (other, next_j)]
+    for row, col in greet:
+        pl.semaphore_signal(
+            barrier, inc=1, device_id={"rows": row, "cols": col},
+            device_id_type=pl.DeviceIdType.MESH,
+        )
+    pl.semaphore_wait(barrier, len(greet))
+
+    targets = ((other, prev_j), (other, j), (i, prev_j))
+    backs = ((other, next_j), (other, j), (i, next_j))
+    quads = [
+        remote(sendq.at[k], winq.at[k], s_q.at[k], r_q.at[k], *targets[k]) for k in range(3)
+    ]
+    for c in quads:
+        c.start()
+    up_rows = pl.ds(pl.multiple_of(i * half, 128), half)
+    merge_out = [
+        remote(w_merge, wm.at[j], s_w.at[0], r_w.at[0], i, far),
+        remote(w_merge, wm.at[j], s_w.at[1], r_w.at[1], i, partner),
+    ]
+    weights_out = [
+        remote(w_up, up.at[up_rows, :], s_w.at[2], r_w.at[2], other, j),
+        remote(w_down, down.at[i], s_w.at[3], r_w.at[3], other, j),
+    ]
+    for c in merge_out + weights_out:
+        c.start()
+    locals_ = [
+        pltpu.make_async_copy(w_merge, wm.at[j], loc.at[0]),
+        pltpu.make_async_copy(w_up, up.at[up_rows, :], loc.at[1]),
+        pltpu.make_async_copy(w_down, down.at[i], loc.at[2]),
+    ]
+    for c in locals_:
+        c.start()
+
+    lane = lax.broadcasted_iota(jnp.int32, (ch, ch), 0) // width
+    lane_t = lax.broadcasted_iota(jnp.int32, (ch, ch), 1) // width
+    block_ones = (lane == lane_t).astype(f32).astype(bf16)
+
+    def unit(value):
+        squares = value * value
+        top = squares.astype(bf16)
+        low = (squares - top.astype(f32)).astype(bf16)
+        total = _dot(top, block_ones) + _dot(low, block_ones)
+        return (value * lax.rsqrt(total + eps_unit)).astype(bf16)
+
+    for c in quads:
+        c.wait_recv()
+    tokens = winq[...].reshape(4 * quad, ch)
+    qhat = unit(_dot(tokens, w_qkv[:, :ch]))
+    khat = unit(_dot(tokens, w_qkv[:, ch:2 * ch]))
+    vals = _dot(tokens, w_qkv[:, 2 * ch:]).astype(bf16)
+    per = 128 // width
+    lanes = lax.broadcasted_iota(jnp.int32, (4 * quad, 128), 1) // width
+    for b in range(ch // 128):
+        cut = slice(b * 128, (b + 1) * 128)
+        qb, kb, vb = qhat[:, cut], khat[:, cut], vals[:, cut]
+        acc = None
+        for t in range(per):
+            mine = lanes == t
+            zero = jnp.zeros_like(qb)
+            scores = _dot(jnp.where(mine, qb, zero), kb, 1, 1) * logit[b * per + t]
+            weights = jnp.exp(scores)
+            weights = (weights / jnp.sum(weights, axis=-1, keepdims=True)).astype(bf16)
+            term = _dot(weights, jnp.where(mine, vb, zero))
+            acc = term if acc is None else acc + term
+        mixw[:, :, cut] = acc.astype(bf16).reshape(4, quad, 128)
+    returns = [
+        remote(mixw.at[k], mixq.at[k], s_b.at[k], r_b.at[k], *backs[k]) for k in range(3)
+    ]
+    for c in returns:
+        c.start()
+    mixq[3] = mixw[3]
+    merge_out[0].wait_recv()
+    onward = remote(wm.at[far], wm.at[far], s_w.at[4], r_w.at[4], i, partner)
+    onward.start()
+    rows_out = lax.broadcasted_iota(jnp.int32, (4 * quad, 4 * quad), 0)
+    cols_in = lax.broadcasted_iota(jnp.int32, (4 * quad, 4 * quad), 1)
+    which, place = rows_out // quad, rows_out % quad
+    r = 2 * (place // half_side) + which % 2
+    c = 2 * (place % half_side) + which // 2
+    source = ((r // half_side) * 2 + c // half_side) * quad + (r % half_side) * half_side + c % half_side
+    permute = (source == cols_in).astype(f32).astype(bf16)
+    for cp in returns:
+        cp.wait_recv()
+    normed, _ = _ln(_dot(mixq[...].reshape(4 * quad, ch), w_proj[...]))
+    flat = jnp.concatenate([quarter(k // 2, k % 2) for k in range(4)], axis=0)
+    stream = (flat + normed).astype(bf16)
+    picked = _dot(permute, stream).astype(bf16)
+    merged = jnp.concatenate([picked[k * quad:(k + 1) * quad] for k in range(4)], axis=1)
+    locals_[0].wait()
+    merge_out[1].wait_recv()
+    onward.wait_recv()
+    projected = jnp.concatenate([_dot(merged, wm[k]) for k in range(nj)], axis=1)
+    level, _ = _ln(projected)
+    lvl[j] = level.astype(bf16)
+    level_out = [
+        remote(lvl.at[j], lvl.at[j], s_l.at[k], r_l.at[k], i, peers[k]) for k in range(3)
+    ]
+    for cp in level_out:
+        cp.start()
+    locals_[1].wait()
+    locals_[2].wait()
+    weights_out[0].wait_recv()
+
+    pair = j // 2
+    pairs = (pair, (pair + 1) % 2)
+
+    def rows_of(p):
+        return pl.ds(pl.multiple_of(p * 2 * own, 128), 2 * own)
+
+    branch_out = []
+    own_rows = None
+    for t in range(2):
+        p = pairs[t]
+        if t == 0:
+            level_out[0].wait_recv()
+        else:
+            level_out[1].wait_recv()
+            level_out[2].wait_recv()
+        pre = _dot(lvl[pl.ds(p * 2, 2)].reshape(2 * own, c4), up[...])
+        cdf = 0.5 * (1.0 + lax.erf(pre * np.float32(np.sqrt(0.5))))
+        hidden = (pre * cdf).astype(bf16)
+        hid[rows_of(p), :] = hidden
+        dgel[rows_of(p), :] = cdf + pre * (jnp.exp(-0.5 * pre * pre) * np.float32(1 / np.sqrt(2 * np.pi)))
+        if t == 0:
+            weights_out[1].wait_recv()
+        out = jnp.concatenate([_dot(hidden, down[k]) for k in range(ni)], axis=1)
+        bsend[pl.ds(p * 2, 2)] = out.astype(bf16).reshape(2, own, c4)
+        for k in ((0,) if t == 0 else (1, 2)):
+            cp = remote(bsend.at[peers[k]], brecv.at[j], s_d.at[k], r_d.at[k], i, peers[k])
+            cp.start()
+            branch_out.append(cp)
+    back_half = pl.ds(pl.multiple_of(other * half, 128), half)
+    my_half = pl.ds(pl.multiple_of(i * half, 128), half)
+    across = [
+        remote(lvl.at[:, :, back_half], lvl_p, s_p.at[0], r_p.at[0], other, j),
+        remote(hid, hid_p, s_p.at[1], r_p.at[1], other, j),
+    ]
+    for cp in across:
+        cp.start()
+    total = bsend[j].astype(f32)
+    for k in range(3):
+        branch_out[k].wait_recv()
+        total = total + brecv[peers[k]].astype(f32)
+    norm, inverse = _ln(total)
+    coarse[...] = level + norm
+    g = cot[...].astype(f32)
+    slope = inverse * (
+        g - jnp.mean(g, axis=-1, keepdims=True) - norm * jnp.mean(g * norm, axis=-1, keepdims=True)
+    )
+    slo[j] = slope.astype(bf16)
+    slope_out = [
+        remote(slo.at[j], slo.at[j], s_s.at[k], r_s.at[k], i, peers[k]) for k in range(3)
+    ]
+    for cp in slope_out:
+        cp.start()
+    grad_out = []
+    for t in range(2):
+        p = pairs[t]
+        if t == 0:
+            slope_out[0].wait_recv()
+        else:
+            slope_out[1].wait_recv()
+            slope_out[2].wait_recv()
+        so = slo[pl.ds(p * 2, 2)].reshape(2 * own, c4)
+        back = _dot(so[:, :half], down[0], 1, 1)
+        for k in range(1, ni):
+            back = back + _dot(so[:, k * half:(k + 1) * half], down[k], 1, 1)
+        sp = (dgel[rows_of(p), :] * back).astype(bf16)
+        spre[rows_of(p), :] = sp
+        out = _dot(sp, up[...], 1, 1)
+        gsend[pl.ds(p * 2, 2)] = out.astype(bf16).reshape(2, own, c4)
+        for k in ((0,) if t == 0 else (1, 2)):
+            cp = remote(gsend.at[peers[k]], grecv.at[j], s_g.at[k], r_g.at[k], i, peers[k])
+            cp.start()
+            grad_out.append(cp)
+    across += [
+        remote(spre, spre_p, s_p.at[3], r_p.at[3], other, j),
+        remote(slo.at[:, :, back_half], slo_p, s_p.at[2], r_p.at[2], other, j),
+    ]
+    across[2].start()
+    across[3].start()
+    hid_all = hid[...]
+    gdown[...] = _dot(hid_all, slo[:, :, my_half].reshape(4 * own, half), 0, 0)
+    gup[...] = _dot(lvl[:, :, my_half].reshape(4 * own, half), spre[...], 0, 0)
+    total = gsend[j].astype(f32)
+    for k in range(3):
+        grad_out[k].wait_recv()
+        total = total + grecv[peers[k]].astype(f32)
+    gcoarse[...] = g + total
+    across[0].wait_recv()
+    across[1].wait_recv()
+    across[3].wait_recv()
+    gdown[...] += _dot(hid_p[...], slo_p[...].reshape(4 * own, half), 0, 0)
+    across[2].wait_recv()
+    gup[...] += _dot(lvl_p[...].reshape(4 * own, half), spre_p[...], 0, 0)
+    sent = quads + merge_out + weights_out + returns + [onward] + level_out
+    for cp in sent + branch_out + slope_out + grad_out + across:
+        cp.wait_send()
+
+
+def fused(fields, logit_scale, w_qkv, w_proj, w_merge, w_up, w_down, cotangent):
+    tile_rows, tile_cols, ch = fields.shape
+    ni, nj = lax.axis_size("rows"), lax.axis_size("cols")
+    own = cotangent.shape[0] * cotangent.shape[1]
+    c4 = cotangent.shape[-1]
+    half, ff = w_up.shape
+    f32, bf16 = jnp.float32, jnp.bfloat16
+    quad = (WIN // 2) ** 2
+    vm = pl.BlockSpec(memory_space=pltpu.VMEM)
+    hb = pl.BlockSpec(memory_space=pl.ANY)
+    dma = pltpu.SemaphoreType.DMA
+    band = nj * own
+    outs = pl.pallas_call(
+        fused_kernel,
+        out_shape=(
+            jax.ShapeDtypeStruct((own, c4), f32),
+            jax.ShapeDtypeStruct((own, c4), f32),
+            jax.ShapeDtypeStruct((half, ff), f32),
+            jax.ShapeDtypeStruct((ff, half), f32),
+        ),
+        in_specs=[vm, pl.BlockSpec(memory_space=pltpu.SMEM), vm, vm, hb, hb, hb, vm],
+        out_specs=(vm, vm, vm, vm),
+        scratch_shapes=[
+            pltpu.VMEM((3, quad, ch), bf16),
+            pltpu.VMEM((4, quad, ch), bf16),
+            pltpu.VMEM((4, quad, ch), bf16),
+            pltpu.VMEM((4, quad, ch), bf16),
+            pltpu.VMEM((nj,) + w_merge.shape, bf16),
+            pltpu.VMEM((c4, ff), bf16),
+            pltpu.VMEM((ni, ff, half), bf16),
+            pltpu.VMEM((nj, own, c4), bf16),
+            pltpu.VMEM((band, ff), bf16),
+            pltpu.VMEM((band, ff), f32),
+            pltpu.VMEM((nj, own, c4), bf16),
+            pltpu.VMEM((nj, own, c4), bf16),
+            pltpu.VMEM((nj, own, c4), bf16),
+            pltpu.VMEM((band, ff), bf16),
+            pltpu.VMEM((nj, own, c4), bf16),
+            pltpu.VMEM((nj, own, c4), bf16),
+            pltpu.VMEM((nj, own, half), bf16),
+            pltpu.VMEM((band, ff), bf16),
+            pltpu.VMEM((nj, own, half), bf16),
+            pltpu.VMEM((band, ff), bf16),
+            dma((3,)),
+            dma((3,)), dma((3,)), dma((3,)), dma((3,)), dma((5,)), dma((5,)),
+            dma((3,)), dma((3,)), dma((3,)), dma((3,)), dma((3,)), dma((3,)),
+            dma((3,)), dma((3,)), dma((4,)), dma((4,)),
+        ],
+        compiler_params=pltpu.CompilerParams(collective_id=0, has_side_effects=True),
+    )(fields, logit_scale, w_qkv, w_proj, w_merge, w_up, w_down, cotangent.reshape(own, c4))
+    shape = (tile_rows // 2, tile_cols // 2, c4)
+    return outs[0].reshape(shape), outs[1].reshape(shape), outs[2], outs[3]
+
+
+def device_body(*args):
+    fields, _, w_qkv, _, w_merge, w_up, w_down, _ = args
+    fits = (
+        lax.axis_size("rows") == 2
+        and lax.axis_size("cols") == 4
+        and fields.shape[:2] == (WIN, WIN)
+        and w_up.shape[0] % 128 == 0
+        and fields.shape[-1] % 128 == 0
+    )
+    return fused(*args) if fits else local(*args)
+
+
 def solution(mesh):
     return jax.shard_map(
-        local,
+        device_body,
         mesh=mesh,
         in_specs=(
             P(("dp", "rows"), "cols", None),

time: 200 us -> 84.2 us (0.42)
  waiting for transfers between devices: 89 us -> 0 us
  Pallas kernels: 0 us -> 74.4 us
  local copies, waits for them, and re-layouts: 32.4 us -> 8.92 us
  blocking collectives: 21.8 us -> 0 us
  matrix products: 19.1 us -> 0 us
  other arithmetic: 17 us -> 0 us
  between operations: 14.5 us -> 0.64 us
  starting transfers between devices: 5.1 us -> 0 us
    pallas_call x0 -> x1, Pallas kernels: none -> 74.4 us  [fused(): pl.pallas_call(fused_kernel, out_shape=(jax.ShapeDtypeStruct((own, c4), f...]
    reduce_scatter x3 -> x0, waiting for transfers between devices: 61.4 us -> none  [the longest x1 22.1 us: local(): lax.psum_scatter(term_up.astype(jnp.bfloat16), 'rows', scatter_dimension=...]
    unnamed x7 -> x0, waiting for transfers between devices: 23.7 us -> none
    all_gather x3 -> x0, blocking collectives: 21.8 us -> none  [the longest x1 9.13 us: local(): lax.all_gather(merged_rows, 'cols', axis=0, tiled=True)]
    dot_general x12 -> x0, matrix products: 19.1 us -> none  [the longest x1 4.33 us: local(): hidden_pre = jnp.dot(level_b, up_full, preferred_element_type=jnp.float32)]
    another operation x6 -> x0, local copies, waits for them, and re-layouts: 13.4 us -> none  [the longest x1 3.78 us: attend(): key_heads = key_rows.reshape(number, window_size, head_count, width_head)]
    convert_element_type x6 -> x0, other arithmetic: 8.03 us -> none  [the longest x2 3.25 us: local(): grad_up, grad_down = (lax.psum_scatter(term_up.astype(jnp.bfloat16), 'row...]
    mul x3 -> x0, local copies, waits for them, and re-layouts: 7.43 us -> none  [the longest x2 4.38 us: unit_heads(): return (shaped * lax.rsqrt(squares + eps_unit)).reshape(value.shape)]
  transfers between devices with their start and end apart: 10 -> 0, of which waited for: 7 -> 0; matrix products, arithmetic and copies ran while one was open for 27% -> 0% of each run, Pallas kernels for 0% -> 0%
where the time goes in v1:
time: 84.2 us; the launch traced here: 84 us
  Pallas kernels  74.4 us (88%)
  local copies, waits for them, and re-layouts  8.92 us (11%)
    pallas_call x1, Pallas kernels, fused(): pl.pallas_call(fused_kernel, out_shape=(jax.ShapeDtypeStruct((own, c4), f...  74.4 us
    unnamed x7, local copies, waits for them, and re-layouts  8.92 us

profile of v1, /device:TPU:0, one launch (start us, length us, event | category | flops | bytes accessed | tf_op | source)
XLA Modules:
  0.0 84.0 jit_solution(13781209789646642548)
XLA Ops:
  0.6 2.2 %copy.12.w_merge = bf16[1536,192]{1,0:T(8,128)(2,1)} copy(bf16[1536,192]{0,1:T(8,128)(2,1)} %param.12) | data formatting | bytes 1179648 | tf_op args[4]
  2.8 74.4 %shard_map.111 = (f32[64,768]{1,0:T(8,128)}, f32[64,768]{1,0:T(8,128)}, f32[384,768]{1,0:T(8,128)}, f32[768,384]{1,0:T(8,128)}) custom-call(f32[16,16,384]{2,1,0:T(8,128)} %fields.1, f32[6]{0:T(128)} %logit.1, bf16[384,1152]{1,0:T(8,128)(2,1)} %w_qkv.1, bf16[384,384]{1,0:T(8,128)(2,1)} %w_proj.1, bf16[1536,192]{1,0:T(8,128)(2,1)} %copy.12.w_merge, ...), custom_call_target="tpu_custom_call" | custom-call | tf_op jit(solution)/shard_map/pallas_call | solution.py:451
  77.3 1.6 %copy.17 = f32[8,8,768]{2,1,0:T(8,128)} copy(f32[8,8,768]{2,1,0:T(8,128)} %bitcast.4) | data formatting | bytes 393216
  78.9 1.6 %copy.18 = f32[8,8,768]{2,1,0:T(8,128)} copy(f32[8,8,768]{2,1,0:T(8,128)} %bitcast.3) | data formatting | bytes 393216
  80.5 0.0 copy-start
  80.5 2.5 %copy.19 = f32[384,768]{1,0:T(8,128)} copy(f32[384,768]{1,0:T(8,128)} %get-tuple-element.18) | data formatting | bytes 2359296
  83.0 0.0 copy-done
  83.0 1.0 %copy.20 = f32[768,384]{1,0:T(8,128)} copy(f32[768,384]{1,0:T(8,128)S(1)} %copy-done) | data formatting | bytes 2359296
Async XLA Ops:
  80.5 2.5 %copy-start = (f32[768,384]{1,0:T(8,128)S(1)}, f32[768,384]{1,0:T(8,128)}, u32[]{:S(2)}) copy-start(f32[768,384]{1,0:T(8,128)} %get-tuple-element.19) | copy-start | bytes 3538948

commit v2 on v1

--- a/solution.py
+++ b/solution.py
@@ -197,14 +197,15 @@
 
 def fused_kernel(
     fields, logit, w_qkv, w_proj, w_merge, w_up, w_down, cot,
-    coarse, gcoarse, gup, gdown,
+    coarse, gcoarse, lvl_o, hid_o, slo_o, spre_o,
     sendq, winq, mixw, mixq, wm, up, down, lvl, hid, dgel, bsend, brecv, slo, spre, gsend, grecv,
-    lvl_p, hid_p, slo_p, spre_p,
     loc, s_q, r_q, s_b, r_b, s_w, r_w, s_l, r_l, s_d, r_d, s_s, r_s, s_g, r_g, s_p, r_p,
 ):
     f32, bf16 = jnp.float32, jnp.bfloat16
     i, j = lax.axis_index("rows"), lax.axis_index("cols")
     ni, nj = lax.axis_size("rows"), lax.axis_size("cols")
+    z = lax.axis_index("dp")
+    beside = z + 1 - 2 * (z % 2)
     half_side = WIN // 2
     quad = half_side * half_side
     ch = fields.shape[-1]
@@ -220,10 +221,11 @@
     far_partner = (partner + 2) % nj
     peers = (partner, far, far_partner)
 
-    def remote(src, dst, send, recv, row, col):
+    def remote(src, dst, send, recv, row, col, part=z):
         return pltpu.make_async_remote_copy(
             src_ref=src, dst_ref=dst, send_sem=send, recv_sem=recv,
-            device_id={"rows": row, "cols": col}, device_id_type=pl.DeviceIdType.MESH,
+            device_id={"rows": row, "cols": col, "dp": part},
+            device_id_type=pl.DeviceIdType.MESH,
         )
 
     def quarter(a, b):
@@ -241,7 +243,10 @@
             barrier, inc=1, device_id={"rows": row, "cols": col},
             device_id_type=pl.DeviceIdType.MESH,
         )
-    pl.semaphore_wait(barrier, len(greet))
+    pl.semaphore_signal(
+        barrier, inc=1, device_id={"dp": beside}, device_id_type=pl.DeviceIdType.MESH
+    )
+    pl.semaphore_wait(barrier, len(greet) + 1)
 
     targets = ((other, prev_j), (other, j), (i, prev_j))
     backs = ((other, next_j), (other, j), (i, next_j))
@@ -250,20 +255,38 @@
     ]
     for c in quads:
         c.start()
-    up_rows = pl.ds(pl.multiple_of(i * half, 128), half)
+    ff = w_up.shape[1]
+    share, wide = w_merge.shape
+    bit = z % 2
+
+    def shard(col):
+        return pl.ds(pl.multiple_of(col * share, 64), share)
+
+    def up_half(row, which):
+        return pl.ds(pl.multiple_of(row * half + which * (half // 2), half // 2), half // 2)
+
+    def down_half(which):
+        return pl.ds(pl.multiple_of(which * (ff // 2), ff // 2), ff // 2)
+
+    def from_half(which):
+        return pl.ds(pl.multiple_of(which * (half // 2), half // 2), half // 2)
+
     merge_out = [
-        remote(w_merge, wm.at[j], s_w.at[0], r_w.at[0], i, far),
-        remote(w_merge, wm.at[j], s_w.at[1], r_w.at[1], i, partner),
+        remote(w_merge, wm.at[shard(j), :], s_w.at[0], r_w.at[0], i, far),
+        remote(w_merge, wm.at[shard(j), :], s_w.at[1], r_w.at[1], i, partner),
     ]
     weights_out = [
-        remote(w_up, up.at[up_rows, :], s_w.at[2], r_w.at[2], other, j),
-        remote(w_down, down.at[i], s_w.at[3], r_w.at[3], other, j),
+        remote(w_up.at[from_half(bit), :], up.at[up_half(i, bit), :], s_w.at[2], r_w.at[2], other, j),
+        remote(
+            w_down.at[down_half(bit), :], down.at[i, down_half(bit), :],
+            s_w.at[3], r_w.at[3], other, j,
+        ),
     ]
     for c in merge_out + weights_out:
         c.start()
     locals_ = [
-        pltpu.make_async_copy(w_merge, wm.at[j], loc.at[0]),
-        pltpu.make_async_copy(w_up, up.at[up_rows, :], loc.at[1]),
+        pltpu.make_async_copy(w_merge, wm.at[shard(j), :], loc.at[0]),
+        pltpu.make_async_copy(w_up, up.at[pl.ds(pl.multiple_of(i * half, half), half), :], loc.at[1]),
         pltpu.make_async_copy(w_down, down.at[i], loc.at[2]),
     ]
     for c in locals_:
@@ -308,8 +331,14 @@
         c.start()
     mixq[3] = mixw[3]
     merge_out[0].wait_recv()
-    onward = remote(wm.at[far], wm.at[far], s_w.at[4], r_w.at[4], i, partner)
+    onward = remote(wm.at[shard(far), :], wm.at[shard(far), :], s_w.at[4], r_w.at[4], i, partner)
     onward.start()
+    weights_out[0].wait_recv()
+    up_on = remote(
+        up.at[up_half(other, bit), :], up.at[up_half(other, bit), :],
+        s_w.at[5], r_w.at[5], i, j, beside,
+    )
+    up_on.start()
     rows_out = lax.broadcasted_iota(jnp.int32, (4 * quad, 4 * quad), 0)
     cols_in = lax.broadcasted_iota(jnp.int32, (4 * quad, 4 * quad), 1)
     which, place = rows_out // quad, rows_out % quad
@@ -327,17 +356,63 @@
     locals_[0].wait()
     merge_out[1].wait_recv()
     onward.wait_recv()
-    projected = jnp.concatenate([_dot(merged, wm[k]) for k in range(nj)], axis=1)
+    projected = _dot(merged, wm[...], 1, 1)
     level, _ = _ln(projected)
     lvl[j] = level.astype(bf16)
-    level_out = [
-        remote(lvl.at[j], lvl.at[j], s_l.at[k], r_l.at[k], i, peers[k]) for k in range(3)
-    ]
-    for cp in level_out:
-        cp.start()
+    back_half = pl.ds(pl.multiple_of(other * half, 128), half)
+    my_half = pl.ds(pl.multiple_of(i * half, 128), half)
+
+    class Gathered:
+        def __init__(self, ref, out, send, recv, p_send, p_recv, base):
+            self.ref, self.out, self.send, self.recv = ref, out, send, recv
+            self.p_send, self.p_recv, self.base = p_send, p_recv, base
+            self.out_far = remote(ref.at[j], ref.at[j], send.at[0], recv.at[0], i, far)
+            self.out_partner = remote(ref.at[j], ref.at[j], send.at[1], recv.at[1], i, partner)
+            self.onward = remote(ref.at[far], ref.at[far], send.at[2], recv.at[2], i, partner)
+            self.across = [
+                remote(
+                    ref.at[s, :, back_half], out.at[1, s],
+                    p_send.at[base + k], p_recv.at[base + k], other, j,
+                )
+                for k, s in enumerate((j, far))
+            ]
+            self.across_on = [
+                remote(
+                    out.at[1, s], out.at[1, s],
+                    p_send.at[base + 2 + k], p_recv.at[base + 2 + k], i, partner,
+                )
+                for k, s in enumerate((j, far))
+            ]
+
+        def start(self):
+            self.out_far.start()
+            self.out_partner.start()
+            self.across[0].start()
+
+        def relay(self):
+            self.out_far.wait_recv()
+            self.onward.start()
+            self.across[1].start()
+
+        def relay_across(self):
+            for k in range(2):
+                self.across[k].wait_recv()
+                self.across_on[k].start()
+
+        def all(self):
+            return [self.out_far, self.out_partner, self.onward] + self.across + self.across_on
+
+    levels = Gathered(lvl, lvl_o, s_l, r_l, s_p, r_p, 0)
+    levels.start()
+    weights_out[1].wait_recv()
+    down_on = remote(
+        down.at[other, down_half(bit), :], down.at[other, down_half(bit), :],
+        s_w.at[6], r_w.at[6], i, j, beside,
+    )
+    down_on.start()
     locals_[1].wait()
     locals_[2].wait()
-    weights_out[0].wait_recv()
+    up_on.wait_recv()
 
     pair = j // 2
     pairs = (pair, (pair + 1) % 2)
@@ -345,35 +420,38 @@
     def rows_of(p):
         return pl.ds(pl.multiple_of(p * 2 * own, 128), 2 * own)
 
-    branch_out = []
+    branch_out, across = [], []
     own_rows = None
     for t in range(2):
         p = pairs[t]
         if t == 0:
-            level_out[0].wait_recv()
+            levels.out_partner.wait_recv()
         else:
-            level_out[1].wait_recv()
-            level_out[2].wait_recv()
+            levels.onward.wait_recv()
         pre = _dot(lvl[pl.ds(p * 2, 2)].reshape(2 * own, c4), up[...])
         cdf = 0.5 * (1.0 + lax.erf(pre * np.float32(np.sqrt(0.5))))
         hidden = (pre * cdf).astype(bf16)
         hid[rows_of(p), :] = hidden
         dgel[rows_of(p), :] = cdf + pre * (jnp.exp(-0.5 * pre * pre) * np.float32(1 / np.sqrt(2 * np.pi)))
         if t == 0:
-            weights_out[1].wait_recv()
+            levels.relay()
+            down_on.wait_recv()
         out = jnp.concatenate([_dot(hidden, down[k]) for k in range(ni)], axis=1)
         bsend[pl.ds(p * 2, 2)] = out.astype(bf16).reshape(2, own, c4)
         for k in ((0,) if t == 0 else (1, 2)):
             cp = remote(bsend.at[peers[k]], brecv.at[j], s_d.at[k], r_d.at[k], i, peers[k])
             cp.start()
             branch_out.append(cp)
-    back_half = pl.ds(pl.multiple_of(other * half, 128), half)
-    my_half = pl.ds(pl.multiple_of(i * half, 128), half)
-    across = [
-        remote(lvl.at[:, :, back_half], lvl_p, s_p.at[0], r_p.at[0], other, j),
-        remote(hid, hid_p, s_p.at[1], r_p.at[1], other, j),
-    ]
-    for cp in across:
+        cp = remote(
+            hid.at[rows_of(p), :], hid_o.at[1, rows_of(p), :], s_p.at[8 + t], r_p.at[8 + t], other, j
+        )
+        cp.start()
+        across.append(cp)
+    keep = [
+        pltpu.make_async_copy(lvl.at[:, :, my_half], lvl_o.at[0], loc.at[3]),
+        pltpu.make_async_copy(hid, hid_o.at[0], loc.at[4]),
+    ]
+    for cp in keep:
         cp.start()
     total = bsend[j].astype(f32)
     for k in range(3):
@@ -386,54 +464,62 @@
         g - jnp.mean(g, axis=-1, keepdims=True) - norm * jnp.mean(g * norm, axis=-1, keepdims=True)
     )
     slo[j] = slope.astype(bf16)
-    slope_out = [
-        remote(slo.at[j], slo.at[j], s_s.at[k], r_s.at[k], i, peers[k]) for k in range(3)
-    ]
-    for cp in slope_out:
-        cp.start()
+    slopes = Gathered(slo, slo_o, s_s, r_s, s_p, r_p, 4)
+    slopes.start()
+    levels.relay_across()
     grad_out = []
     for t in range(2):
         p = pairs[t]
         if t == 0:
-            slope_out[0].wait_recv()
+            slopes.out_partner.wait_recv()
         else:
-            slope_out[1].wait_recv()
-            slope_out[2].wait_recv()
+            slopes.onward.wait_recv()
         so = slo[pl.ds(p * 2, 2)].reshape(2 * own, c4)
         back = _dot(so[:, :half], down[0], 1, 1)
         for k in range(1, ni):
             back = back + _dot(so[:, k * half:(k + 1) * half], down[k], 1, 1)
         sp = (dgel[rows_of(p), :] * back).astype(bf16)
         spre[rows_of(p), :] = sp
+        if t == 0:
+            slopes.relay()
+        cp = remote(
+            spre.at[rows_of(p), :], spre_o.at[1, rows_of(p), :],
+            s_p.at[10 + t], r_p.at[10 + t], other, j,
+        )
+        cp.start()
+        across.append(cp)
         out = _dot(sp, up[...], 1, 1)
         gsend[pl.ds(p * 2, 2)] = out.astype(bf16).reshape(2, own, c4)
         for k in ((0,) if t == 0 else (1, 2)):
             cp = remote(gsend.at[peers[k]], grecv.at[j], s_g.at[k], r_g.at[k], i, peers[k])
             cp.start()
             grad_out.append(cp)
-    across += [
-        remote(spre, spre_p, s_p.at[3], r_p.at[3], other, j),
-        remote(slo.at[:, :, back_half], slo_p, s_p.at[2], r_p.at[2], other, j),
-    ]
-    across[2].start()
-    across[3].start()
-    hid_all = hid[...]
-    gdown[...] = _dot(hid_all, slo[:, :, my_half].reshape(4 * own, half), 0, 0)
-    gup[...] = _dot(lvl[:, :, my_half].reshape(4 * own, half), spre[...], 0, 0)
+    keep += [
+        pltpu.make_async_copy(slo.at[:, :, my_half], slo_o.at[0], loc.at[5]),
+        pltpu.make_async_copy(spre, spre_o.at[0], loc.at[6]),
+    ]
+    keep[2].start()
+    keep[3].start()
+    slopes.relay_across()
     total = gsend[j].astype(f32)
     for k in range(3):
         grad_out[k].wait_recv()
         total = total + grecv[peers[k]].astype(f32)
     gcoarse[...] = g + total
-    across[0].wait_recv()
-    across[1].wait_recv()
-    across[3].wait_recv()
-    gdown[...] += _dot(hid_p[...], slo_p[...].reshape(4 * own, half), 0, 0)
-    across[2].wait_recv()
-    gup[...] += _dot(lvl_p[...].reshape(4 * own, half), spre_p[...], 0, 0)
-    sent = quads + merge_out + weights_out + returns + [onward] + level_out
-    for cp in sent + branch_out + slope_out + grad_out + across:
+    for cp in levels.across_on + slopes.across_on + across:
+        cp.wait_recv()
+    for cp in keep:
+        cp.wait()
+    sent = quads + merge_out + weights_out + returns + [onward, up_on, down_on]
+    for cp in sent + levels.all() + branch_out + slopes.all() + grad_out + across:
         cp.wait_send()
+
+
+def weight_kernel(coarse_in, gcoarse_in, lvl, hid, slo, spre, coarse, gcoarse, gup, gdown):
+    coarse[...] = coarse_in[...]
+    gcoarse[...] = gcoarse_in[...]
+    gup[...] = _dot(lvl[...], spre[...], 0, 0)
+    gdown[...] = _dot(hid[...], slo[...], 0, 0)
 
 
 def fused(fields, logit_scale, w_qkv, w_proj, w_merge, w_up, w_down, cotangent):
@@ -448,22 +534,24 @@
     hb = pl.BlockSpec(memory_space=pl.ANY)
     dma = pltpu.SemaphoreType.DMA
     band = nj * own
+    acts = (
+        jax.ShapeDtypeStruct((ni, nj, own, half), bf16),
+        jax.ShapeDtypeStruct((ni, band, ff), bf16),
+        jax.ShapeDtypeStruct((ni, nj, own, half), bf16),
+        jax.ShapeDtypeStruct((ni, band, ff), bf16),
+    )
+    grid = (jax.ShapeDtypeStruct((own, c4), f32),) * 2
     outs = pl.pallas_call(
         fused_kernel,
-        out_shape=(
-            jax.ShapeDtypeStruct((own, c4), f32),
-            jax.ShapeDtypeStruct((own, c4), f32),
-            jax.ShapeDtypeStruct((half, ff), f32),
-            jax.ShapeDtypeStruct((ff, half), f32),
-        ),
+        out_shape=grid + acts,
         in_specs=[vm, pl.BlockSpec(memory_space=pltpu.SMEM), vm, vm, hb, hb, hb, vm],
-        out_specs=(vm, vm, vm, vm),
+        out_specs=(vm, vm, hb, hb, hb, hb),
         scratch_shapes=[
             pltpu.VMEM((3, quad, ch), bf16),
             pltpu.VMEM((4, quad, ch), bf16),
             pltpu.VMEM((4, quad, ch), bf16),
             pltpu.VMEM((4, quad, ch), bf16),
-            pltpu.VMEM((nj,) + w_merge.shape, bf16),
+            pltpu.VMEM((c4, w_merge.shape[0]), bf16),
             pltpu.VMEM((c4, ff), bf16),
             pltpu.VMEM((ni, ff, half), bf16),
             pltpu.VMEM((nj, own, c4), bf16),
@@ -475,17 +563,25 @@
             pltpu.VMEM((band, ff), bf16),
             pltpu.VMEM((nj, own, c4), bf16),
             pltpu.VMEM((nj, own, c4), bf16),
-            pltpu.VMEM((nj, own, half), bf16),
-            pltpu.VMEM((band, ff), bf16),
-            pltpu.VMEM((nj, own, half), bf16),
-            pltpu.VMEM((band, ff), bf16),
-            dma((3,)),
-            dma((3,)), dma((3,)), dma((3,)), dma((3,)), dma((5,)), dma((5,)),
+            dma((7,)),
+            dma((3,)), dma((3,)), dma((3,)), dma((3,)), dma((7,)), dma((7,)),
             dma((3,)), dma((3,)), dma((3,)), dma((3,)), dma((3,)), dma((3,)),
-            dma((3,)), dma((3,)), dma((4,)), dma((4,)),
+            dma((3,)), dma((3,)), dma((12,)), dma((12,)),
         ],
         compiler_params=pltpu.CompilerParams(collective_id=0, has_side_effects=True),
-    )(fields, logit_scale, w_qkv, w_proj, w_merge, w_up, w_down, cotangent.reshape(own, c4))
+    )(fields, logit_scale, w_qkv, w_proj, w_merge.T, w_up, w_down, cotangent.reshape(own, c4))
+    tokens = ni * band
+    flat = (
+        outs[0], outs[1], outs[2].reshape(tokens, half), outs[3].reshape(tokens, ff),
+        outs[4].reshape(tokens, half), outs[5].reshape(tokens, ff),
+    )
+    outs = pl.pallas_call(
+        weight_kernel,
+        out_shape=grid
+        + (jax.ShapeDtypeStruct((half, ff), f32), jax.ShapeDtypeStruct((ff, half), f32)),
+        in_specs=[vm] * 6,
+        out_specs=(vm,) * 4,
+    )(*flat)
     shape = (tile_rows // 2, tile_cols // 2, c4)
     return outs[0].reshape(shape), outs[1].reshape(shape), outs[2], outs[3]
 
@@ -495,6 +591,7 @@
     fits = (
         lax.axis_size("rows") == 2
         and lax.axis_size("cols") == 4
+        and lax.axis_size("dp") % 2 == 0
         and fields.shape[:2] == (WIN, WIN)
         and w_up.shape[0] % 128 == 0
         and fields.shape[-1] % 128 == 0

time: 84.2 us -> 63.5 us (0.75)
  Pallas kernels: 74.4 us -> 62.7 us
  local copies, waits for them, and re-layouts: 8.92 us -> 0 us
    pallas_call x1 -> x2, Pallas kernels: 74.4 us -> 62.7 us  [the longest x1 58.5 us: fused(): pl.pallas_call(fused_kernel, out_shape=grid + acts, in_specs=[vm, pl.Bloc...]
    unnamed x7 -> x0, local copies, waits for them, and re-layouts: 8.92 us -> none
where the time goes in v2:
time: 63.5 us; the launch traced here: 63.3 us
  Pallas kernels  62.7 us (99%)
  between operations  0.64 us (1%)
    pallas_call x1, Pallas kernels, fused(): pl.pallas_call(fused_kernel, out_shape=grid + acts, in_specs=[vm, pl.Bloc...  58.5 us
    pallas_call x1, Pallas kernels, fused(): pl.pallas_call(weight_kernel, out_shape=grid + (jax.ShapeDtypeStruct((hal...  4.16 us

profile of v2, /device:TPU:0, one launch (start us, length us, event | category | flops | bytes accessed | tf_op | source)
XLA Modules:
  0.0 63.3 jit_solution(9487031185194915964)
XLA Ops:
  0.6 58.5 %shard_map.111 = (f32[64,768]{1,0:T(8,128)}, f32[64,768]{1,0:T(8,128)}, bf16[2,4,64,384]{3,2,1,0:T(8,128)(2,1)}, bf16[2,256,768]{2,1,0:T(8,128)(2,1)}, bf16[2,4,...) custom-call(f32[16,16,384]{2,1,0:T(8,128)} %fields.1, f32[6]{0:T(128)} %logit.1, bf16[384,1152]{1,0:T(8,128)(2,1)} %w_qkv.1, ...), custom_call_target="tpu_custom_call" | custom-call | tf_op jit(solution)/shard_map/pallas_call | solution.py:544
  59.1 4.2 %shard_map.112 = (f32[64,768]{1,0:T(8,128)}, f32[64,768]{1,0:T(8,128)}, f32[384,768]{1,0:T(8,128)}, f32[768,384]{1,0:T(8,128)}) custom-call(f32[64,768]{1,0:T(8,128)} %get-tuple-element.14.coarse_in, f32[64,768]{1,0:T(8,128)} %get-tuple-element.15.gcoarse_in, bf16[512,384]{1,0:T(8,128)(2,1)} %bitcast.11, bf16[512,768]{1,0:T(8,128)(2,1)} %bitcast.8, ...), custom_call_target="tpu_custom_call" | custom-call | tf_op jit(solution)/shard_map/pallas_call | solution.py:578

commit v3 on v2

--- a/solution.py
+++ b/solution.py
@@ -262,27 +262,61 @@
     def shard(col):
         return pl.ds(pl.multiple_of(col * share, 64), share)
 
-    def up_half(row, which):
-        return pl.ds(pl.multiple_of(row * half + which * (half // 2), half // 2), half // 2)
-
-    def down_half(which):
-        return pl.ds(pl.multiple_of(which * (ff // 2), ff // 2), ff // 2)
-
-    def from_half(which):
-        return pl.ds(pl.multiple_of(which * (half // 2), half // 2), half // 2)
-
-    merge_out = [
-        remote(w_merge, wm.at[shard(j), :], s_w.at[0], r_w.at[0], i, far),
-        remote(w_merge, wm.at[shard(j), :], s_w.at[1], r_w.at[1], i, partner),
-    ]
-    weights_out = [
-        remote(w_up.at[from_half(bit), :], up.at[up_half(i, bit), :], s_w.at[2], r_w.at[2], other, j),
+    def piece(start, size, part):
+        return pl.ds(pl.multiple_of(start + part * (size // 2), size // 2), size // 2)
+
+    def up_rows(row, part):
+        return piece(row * half + bit * (half // 2), half // 2, part)
+
+    def down_rows(part):
+        return piece(bit * (ff // 2), ff // 2, part)
+
+    def merge_rows(col, part):
+        return piece(col * share, share, part)
+
+    merge_far = [
         remote(
-            w_down.at[down_half(bit), :], down.at[i, down_half(bit), :],
-            s_w.at[3], r_w.at[3], other, j,
-        ),
-    ]
-    for c in merge_out + weights_out:
+            w_merge.at[piece(0, share, q), :], wm.at[merge_rows(j, q), :],
+            s_w.at[q], r_w.at[q], i, far,
+        )
+        for q in range(2)
+    ]
+    merge_on = [
+        remote(
+            wm.at[merge_rows(far, q), :], wm.at[merge_rows(far, q), :],
+            s_w.at[2 + q], r_w.at[2 + q], i, partner,
+        )
+        for q in range(2)
+    ]
+    merge_beside = remote(w_merge, wm.at[shard(j), :], s_w.at[4], r_w.at[4], i, partner)
+    up_out = [
+        remote(
+            w_up.at[up_rows(0, q), :], up.at[up_rows(i, q), :], s_w.at[5 + q], r_w.at[5 + q], other, j
+        )
+        for q in range(2)
+    ]
+    up_on = [
+        remote(
+            up.at[up_rows(other, q), :], up.at[up_rows(other, q), :],
+            s_w.at[7 + q], r_w.at[7 + q], i, j, beside,
+        )
+        for q in range(2)
+    ]
+    down_out = [
+        remote(
+            w_down.at[down_rows(q), :], down.at[i, down_rows(q), :],
+            s_w.at[9 + q], r_w.at[9 + q], other, j,
+        )
+        for q in range(2)
+    ]
+    down_on = [
+        remote(
+            down.at[other, down_rows(q), :], down.at[other, down_rows(q), :],
+            s_w.at[11 + q], r_w.at[11 + q], i, j, beside,
+        )
+        for q in range(2)
+    ]
+    for c in (up_out[0], merge_far[0], merge_beside, up_out[1]):
         c.start()
     locals_ = [
         pltpu.make_async_copy(w_merge, wm.at[shard(j), :], loc.at[0]),
@@ -309,6 +343,8 @@
     qhat = unit(_dot(tokens, w_qkv[:, :ch]))
     khat = unit(_dot(tokens, w_qkv[:, ch:2 * ch]))
     vals = _dot(tokens, w_qkv[:, 2 * ch:]).astype(bf16)
+    up_out[0].wait_recv()
+    up_on[0].start()
     per = 128 // width
     lanes = lax.broadcasted_iota(jnp.int32, (4 * quad, 128), 1) // width
     for b in range(ch // 128):
@@ -329,16 +365,13 @@
     ]
     for c in returns:
         c.start()
+    for c in (merge_far[1], down_out[0], down_out[1]):
+        c.start()
     mixq[3] = mixw[3]
-    merge_out[0].wait_recv()
-    onward = remote(wm.at[shard(far), :], wm.at[shard(far), :], s_w.at[4], r_w.at[4], i, partner)
-    onward.start()
-    weights_out[0].wait_recv()
-    up_on = remote(
-        up.at[up_half(other, bit), :], up.at[up_half(other, bit), :],
-        s_w.at[5], r_w.at[5], i, j, beside,
-    )
-    up_on.start()
+    up_out[1].wait_recv()
+    up_on[1].start()
+    merge_far[0].wait_recv()
+    merge_on[0].start()
     rows_out = lax.broadcasted_iota(jnp.int32, (4 * quad, 4 * quad), 0)
     cols_in = lax.broadcasted_iota(jnp.int32, (4 * quad, 4 * quad), 1)
     which, place = rows_out // quad, rows_out % quad
@@ -354,8 +387,12 @@
     picked = _dot(permute, stream).astype(bf16)
     merged = jnp.concatenate([picked[k * quad:(k + 1) * quad] for k in range(4)], axis=1)
     locals_[0].wait()
-    merge_out[1].wait_recv()
-    onward.wait_recv()
+    down_out[0].wait_recv()
+    down_on[0].start()
+    merge_far[1].wait_recv()
+    merge_on[1].start()
+    for c in (merge_beside, merge_on[0], merge_on[1]):
+        c.wait_recv()
     projected = _dot(merged, wm[...], 1, 1)
     level, _ = _ln(projected)
     lvl[j] = level.astype(bf16)
@@ -404,15 +441,12 @@
 
     levels = Gathered(lvl, lvl_o, s_l, r_l, s_p, r_p, 0)
     levels.start()
-    weights_out[1].wait_recv()
-    down_on = remote(
-        down.at[other, down_half(bit), :], down.at[other, down_half(bit), :],
-        s_w.at[6], r_w.at[6], i, j, beside,
-    )
-    down_on.start()
+    down_out[1].wait_recv()
+    down_on[1].start()
     locals_[1].wait()
     locals_[2].wait()
-    up_on.wait_recv()
+    up_on[0].wait_recv()
+    up_on[1].wait_recv()
 
     pair = j // 2
     pairs = (pair, (pair + 1) % 2)
@@ -435,7 +469,8 @@
         dgel[rows_of(p), :] = cdf + pre * (jnp.exp(-0.5 * pre * pre) * np.float32(1 / np.sqrt(2 * np.pi)))
         if t == 0:
             levels.relay()
-            down_on.wait_recv()
+            down_on[0].wait_recv()
+            down_on[1].wait_recv()
         out = jnp.concatenate([_dot(hidden, down[k]) for k in range(ni)], axis=1)
         bsend[pl.ds(p * 2, 2)] = out.astype(bf16).reshape(2, own, c4)
         for k in ((0,) if t == 0 else (1, 2)):
@@ -510,7 +545,8 @@
         cp.wait_recv()
     for cp in keep:
         cp.wait()
-    sent = quads + merge_out + weights_out + returns + [onward, up_on, down_on]
+    weights = merge_far + merge_on + [merge_beside] + up_out + up_on + down_out + down_on
+    sent = quads + weights + returns
     for cp in sent + levels.all() + branch_out + slopes.all() + grad_out + across:
         cp.wait_send()
 
@@ -564,7 +600,7 @@
             pltpu.VMEM((nj, own, c4), bf16),
             pltpu.VMEM((nj, own, c4), bf16),
             dma((7,)),
-            dma((3,)), dma((3,)), dma((3,)), dma((3,)), dma((7,)), dma((7,)),
+            dma((3,)), dma((3,)), dma((3,)), dma((3,)), dma((13,)), dma((13,)),
             dma((3,)), dma((3,)), dma((3,)), dma((3,)), dma((3,)), dma((3,)),
             dma((3,)), dma((3,)), dma((12,)), dma((12,)),
         ],

time: 63.5 us -> 60.5 us (0.953)
  Pallas kernels: 62.7 us -> 59.7 us
    pallas_call x1, Pallas kernels: 58.5 us -> 55.5 us  [fused(): pl.pallas_call(fused_kernel, out_shape=grid + acts, in_specs=[vm, pl.Bloc...]
where the time goes in v3:
time: 60.5 us; the launch traced here: 60.3 us
  Pallas kernels  59.7 us (99%)
  between operations  0.64 us (1%)
    pallas_call x1, Pallas kernels, fused(): pl.pallas_call(fused_kernel, out_shape=grid + acts, in_specs=[vm, pl.Bloc...  55.5 us
    pallas_call x1, Pallas kernels, fused(): pl.pallas_call(weight_kernel, out_shape=grid + (jax.ShapeDtypeStruct((hal...  4.16 us

profile of v3, /device:TPU:0, one launch (start us, length us, event | category | flops | bytes accessed | tf_op | source)
XLA Modules:
  0.0 60.3 jit_solution(13551703272480331966)
XLA Ops:
  0.6 55.5 %shard_map.111 = (f32[64,768]{1,0:T(8,128)}, f32[64,768]{1,0:T(8,128)}, bf16[2,4,64,384]{3,2,1,0:T(8,128)(2,1)}, bf16[2,256,768]{2,1,0:T(8,128)(2,1)}, bf16[2,4,...) custom-call(f32[16,16,384]{2,1,0:T(8,128)} %fields.1, f32[6]{0:T(128)} %logit.1, bf16[384,1152]{1,0:T(8,128)(2,1)} %w_qkv.1, ...), custom_call_target="tpu_custom_call" | custom-call | tf_op jit(solution)/shard_map/pallas_call | solution.py:580
  56.2 4.2 %shard_map.112 = (f32[64,768]{1,0:T(8,128)}, f32[64,768]{1,0:T(8,128)}, f32[384,768]{1,0:T(8,128)}, f32[768,384]{1,0:T(8,128)}) custom-call(f32[64,768]{1,0:T(8,128)} %get-tuple-element.14.coarse_in, f32[64,768]{1,0:T(8,128)} %get-tuple-element.15.gcoarse_in, bf16[512,384]{1,0:T(8,128)(2,1)} %bitcast.11, bf16[512,768]{1,0:T(8,128)(2,1)} %bitcast.8, ...), custom_call_target="tpu_custom_call" | custom-call | tf_op jit(solution)/shard_map/pallas_call | solution.py:614

commit v4 on v3

--- a/solution.py
+++ b/solution.py
@@ -473,10 +473,11 @@
             down_on[1].wait_recv()
         out = jnp.concatenate([_dot(hidden, down[k]) for k in range(ni)], axis=1)
         bsend[pl.ds(p * 2, 2)] = out.astype(bf16).reshape(2, own, c4)
-        for k in ((0,) if t == 0 else (1, 2)):
-            cp = remote(bsend.at[peers[k]], brecv.at[j], s_d.at[k], r_d.at[k], i, peers[k])
-            cp.start()
-            branch_out.append(cp)
+        cp = remote(
+            bsend.at[(partner, far_partner)[t]], brecv.at[t], s_d.at[t], r_d.at[t], i, partner
+        )
+        cp.start()
+        branch_out.append(cp)
         cp = remote(
             hid.at[rows_of(p), :], hid_o.at[1, rows_of(p), :], s_p.at[8 + t], r_p.at[8 + t], other, j
         )
@@ -488,10 +489,14 @@
     ]
     for cp in keep:
         cp.start()
-    total = bsend[j].astype(f32)
-    for k in range(3):
-        branch_out[k].wait_recv()
-        total = total + brecv[peers[k]].astype(f32)
+    branch_out[1].wait_recv()
+    brecv[3] = (bsend[far].astype(f32) + brecv[1].astype(f32)).astype(bf16)
+    branch_out.append(remote(brecv.at[3], brecv.at[2], s_d.at[2], r_d.at[2], i, far))
+    branch_out[2].start()
+    branch_out[0].wait_recv()
+    total = bsend[j].astype(f32) + brecv[0].astype(f32)
+    branch_out[2].wait_recv()
+    total = total + brecv[2].astype(f32)
     norm, inverse = _ln(total)
     coarse[...] = level + norm
     g = cot[...].astype(f32)

time: 60.5 us -> 58.6 us (0.969)
  Pallas kernels: 59.7 us -> 57.7 us
    pallas_call x1, Pallas kernels: 55.5 us -> 53.6 us  [fused(): pl.pallas_call(fused_kernel, out_shape=grid + acts, in_specs=[vm, pl.Bloc...]
where the time goes in v4:
time: 58.6 us; the launch traced here: 58.4 us
  Pallas kernels  57.7 us (98%)
  between operations  0.64 us (1%)
    pallas_call x1, Pallas kernels, fused(): pl.pallas_call(fused_kernel, out_shape=grid + acts, in_specs=[vm, pl.Bloc...  53.6 us
    pallas_call x1, Pallas kernels, fused(): pl.pallas_call(weight_kernel, out_shape=grid + (jax.ShapeDtypeStruct((hal...  4.16 us

profile of v4, /device:TPU:0, one launch (start us, length us, event | category | flops | bytes accessed | tf_op | source)
XLA Modules:
  0.0 58.4 jit_solution(11664802991237239100)
XLA Ops:
  0.6 53.6 %shard_map.111 = (f32[64,768]{1,0:T(8,128)}, f32[64,768]{1,0:T(8,128)}, bf16[2,4,64,384]{3,2,1,0:T(8,128)(2,1)}, bf16[2,256,768]{2,1,0:T(8,128)(2,1)}, bf16[2,4,...) custom-call(f32[16,16,384]{2,1,0:T(8,128)} %fields.1, f32[6]{0:T(128)} %logit.1, bf16[384,1152]{1,0:T(8,128)(2,1)} %w_qkv.1, ...), custom_call_target="tpu_custom_call" | custom-call | tf_op jit(solution)/shard_map/pallas_call | solution.py:585
  54.2 4.2 %shard_map.112 = (f32[64,768]{1,0:T(8,128)}, f32[64,768]{1,0:T(8,128)}, f32[384,768]{1,0:T(8,128)}, f32[768,384]{1,0:T(8,128)}) custom-call(f32[64,768]{1,0:T(8,128)} %get-tuple-element.14.coarse_in, f32[64,768]{1,0:T(8,128)} %get-tuple-element.15.gcoarse_in, bf16[512,384]{1,0:T(8,128)(2,1)} %bitcast.11, bf16[512,768]{1,0:T(8,128)(2,1)} %bitcast.8, ...), custom_call_target="tpu_custom_call" | custom-call | tf_op jit(solution)/shard_map/pallas_call | solution.py:619
